TPU v7x, 32 devices: a whole 2x2x4 slice. The times are simulated.
32 devices in a mesh: dp: 32 (over z, y, x, core).
Axes of the slice: x: 2, y: 2, z: 4, core: 2. Of those that a mesh axis runs over, the one named last changes fastest.
Arguments:
- tokens: bfloat16 [16384, 768], P('dp'), may hold values from -6 to 6
- cotangent: bfloat16 [16384, 768], P('dp'), may hold values from -15 to 15
- seq_lengths: int32 [32, 2], P('dp'), may hold values from 0 to 512, as said below
- random_feat: bfloat16 [12, 64, 64], replicated, may hold values from -4 to 4
- w_qkv: float32 [768, 2304], P('dp'), may hold values from -0.21875 to 0.21875
- b_qkv: float32 [2304], P('dp'), may hold values from -1.5 to 1.5
- w_out: float32 [768, 768], P('dp'), may hold values from -0.875 to 0.875
- b_out: float32 [768], P('dp'), may hold values from -1.5 to 1.5
- ln1_gain: float32 [768], P('dp'), may hold values from 0.25 to 1.75
- ln1_bias: float32 [768], P('dp'), may hold values from -1.5 to 1.5
- w_up: float32 [768, 3072], P('dp'), may hold values from -0.21875 to 0.21875
- b_up: float32 [3072], P('dp'), may hold values from -1.5 to 1.5
- w_down: float32 [3072, 768], P('dp'), may hold values from -0.109375 to 0.109375
- b_down: float32 [768], P('dp'), may hold values from -1.5 to 1.5
- ln2_gain: float32 [768], P('dp'), may hold values from 0.25 to 1.75
- ln2_bias: float32 [768], P('dp'), may hold values from -1.5 to 1.5
- rpe_table: float32 [12288], P('dp'), may hold values from -2.5 to 2.5
Outputs:
- out: bfloat16 [16384, 768], P('dp')
- grad_tokens: float32 [16384, 768], P('dp')
- grad_w_qkv: float32 [768, 2304], P('dp')
- grad_b_qkv: float32 [2304], P('dp')
- grad_w_out: float32 [768, 768], P('dp')
- grad_b_out: float32 [768], P('dp')
- grad_ln1_gain: float32 [768], P('dp')
- grad_ln1_bias: float32 [768], P('dp')
- grad_w_up: float32 [768, 3072], P('dp')
- grad_b_up: float32 [3072], P('dp')
- grad_w_down: float32 [3072, 768], P('dp')
- grad_b_down: float32 [768], P('dp')
- grad_ln2_gain: float32 [768], P('dp')
- grad_ln2_bias: float32 [768], P('dp')
- grad_rpe: float32 [12288], P('dp')
Inputs may be any that keep to these rules, and one draw needn't show every extreme that they name: `seq_lengths`: row n gives the lengths of the one or two sequences packed from the start of device n's 512 token slots; a second length of 0 means one sequence; the two lengths sum to 512 or less, and some row holds one sequence of exactly 512.
All inputs are finite; a program needn't handle non-finite values.
Results may differ from a plain program's by a relative error of at most 0.018.
Values may be sent and summed in bfloat16 or wider, within the bound.
A program may use at most 192 MiB of HBM per device.

v0:
```python
import jax
import jax.numpy as jnp
from jax import lax
from jax.sharding import PartitionSpec as P

EPSILON = 1e-05
HIGHEST = lax.Precision.HIGHEST


def to_low(value):
    return value.astype(jnp.bfloat16)


def contract(first_op, second_op, first_dim, second_dim):
    return lax.dot_general(
        first_op,
        second_op,
        (((first_dim,), (second_dim,)), ((), ())),
        preferred_element_type=jnp.float32,
    )


def layer_norm(value, gain, offset):
    centred = value - jnp.mean(value, axis=-1, keepdims=True)
    inverse = lax.rsqrt(jnp.mean(centred * centred, axis=-1, keepdims=True) + EPSILON)
    return centred * inverse * gain + offset


def feature_map(part, projection):
    head_size = part.shape[-1]
    scaled = part * head_size ** (-0.25)
    mapped = jnp.einsum("thd,hdm->thm", scaled, projection, precision=HIGHEST)
    squared = 0.5 * jnp.sum(scaled * scaled, axis=-1, keepdims=True)
    return jnp.exp(mapped - squared) * projection.shape[-1] ** (-0.5)


def exact_gelu(value):
    return jax.nn.gelu(value, approximate=False)


def toeplitz_block(vector, height, breadth):
    tiled = jnp.broadcast_to(vector[::-1], (height, height + breadth - 1)).reshape(-1)
    padded = jnp.concatenate([tiled, jnp.zeros((height,), vector.dtype)])
    return padded.reshape(height, height + breadth)[:, :breadth][::-1]


def diagonal_sums(matrix):
    height, breadth = matrix.shape
    widened = jnp.concatenate(
        [matrix[::-1], jnp.zeros((height, height), matrix.dtype)], axis=1
    ).reshape(-1)
    skewed = widened[: height * (height + breadth - 1)].reshape(height, height + breadth - 1)
    return jnp.sum(skewed, axis=0)[::-1]


def block_kernel(query_feat, key_feat, coef_row, segment, start, block_rows):
    row_count = key_feat.shape[0]
    half_span = coef_row.shape[0] // 2
    window = coef_row[start + half_span - row_count + 1 : start + block_rows + half_span]
    coefficient = toeplitz_block(window, block_rows, row_count)
    kernel = contract(query_feat, key_feat, 1, 1)
    same = segment[start : start + block_rows, None] == segment[None, :]
    return (kernel, coefficient, same)


def head_forward(query_feat, key_feat, values, coef_row, segment, block_rows):
    kernel, coefficient, same = block_kernel(query_feat, key_feat, coef_row, segment, 0, block_rows)
    scores = jnp.where(same, kernel * coefficient, 0.0)
    denominator = jnp.sum(scores, axis=1)
    numerator = jnp.dot(to_low(scores), values, preferred_element_type=jnp.float32)
    contexts = [numerator / denominator[:, None]]
    totals = [denominator]
    return (jnp.concatenate(contexts, axis=0), jnp.concatenate(totals, axis=0))


def head_backward(
    query_feat, key_feat, values, coef_row, segment, context, denominator, grad_context, block_rows
):
    row_count = key_feat.shape[0]
    span = coef_row.shape[0]
    half_span = span // 2
    grad_keys = jnp.zeros(key_feat.shape, jnp.float32)
    grad_values = jnp.zeros(values.shape, jnp.float32)
    grad_coef = jnp.zeros((span,), jnp.float32)
    kernel, coefficient, same = block_kernel(query_feat, key_feat, coef_row, segment, 0, block_rows)
    scores = jnp.where(same, kernel * coefficient, 0.0)
    grad_numer = to_low(grad_context / denominator[0:block_rows, None])
    grad_denom = -jnp.sum(grad_context * context[0:block_rows], axis=1) / denominator[0:block_rows]
    grad_scores = jnp.where(same, contract(grad_numer, values, 1, 1) + grad_denom[:, None], 0.0)
    grad_kernel = to_low(grad_scores * coefficient)
    lowest = half_span - row_count + 1
    grad_coef = grad_coef.at[lowest : block_rows + half_span].add(
        diagonal_sums(grad_scores * kernel)
    )
    grad_queries = [jnp.dot(grad_kernel, key_feat, preferred_element_type=jnp.float32)]
    grad_keys = grad_keys + contract(grad_kernel, query_feat, 0, 0)
    grad_values = grad_values + contract(to_low(scores), grad_numer, 0, 0)
    return (jnp.concatenate(grad_queries, axis=0), grad_keys, grad_values, grad_coef * coef_row)


def body(
    tokens,
    cotangent,
    seq_lengths,
    random_feat,
    w_qkv,
    b_qkv,
    w_out,
    b_out,
    ln1_gain,
    ln1_bias,
    w_up,
    b_up,
    w_down,
    b_down,
    ln2_gain,
    ln2_bias,
    rpe_table,
):
    row_count, breadth = tokens.shape
    heads, head_size, feature_count = random_feat.shape
    block_rows = min(512, row_count)
    position = jnp.arange(row_count, dtype=jnp.int32)
    first_end = seq_lengths[0, 0]
    second_end = first_end + seq_lengths[0, 1]
    segment = (position >= first_end).astype(jnp.int32) + (position >= second_end).astype(jnp.int32)
    valid = (position < second_end).astype(jnp.float32)
    projection = random_feat.astype(jnp.float32)
    (
        full_qkv,
        full_qkv_bias,
        full_out,
        full_out_bias,
        full_gain_one,
        full_bias_one,
        full_up,
        full_up_bias,
        full_down,
        full_down_bias,
        full_gain_two,
        full_bias_two,
        full_rpe,
    ) = (
        lax.all_gather(to_low(w_qkv), "dp", axis=0, tiled=True),
        lax.all_gather(to_low(b_qkv), "dp", axis=0, tiled=True),
        lax.all_gather(to_low(w_out), "dp", axis=0, tiled=True),
        lax.all_gather(to_low(b_out), "dp", axis=0, tiled=True),
        lax.all_gather(to_low(ln1_gain), "dp", axis=0, tiled=True),
        lax.all_gather(to_low(ln1_bias), "dp", axis=0, tiled=True),
        lax.all_gather(to_low(w_up), "dp", axis=0, tiled=True),
        lax.all_gather(to_low(b_up), "dp", axis=0, tiled=True),
        lax.all_gather(to_low(w_down), "dp", axis=0, tiled=True),
        lax.all_gather(to_low(b_down), "dp", axis=0, tiled=True),
        lax.all_gather(to_low(ln2_gain), "dp", axis=0, tiled=True),
        lax.all_gather(to_low(ln2_bias), "dp", axis=0, tiled=True),
        lax.all_gather(to_low(rpe_table), "dp", axis=0, tiled=True),
    )
    span = full_rpe.shape[0] // heads
    qkv = jnp.dot(tokens, full_qkv, preferred_element_type=jnp.float32) + full_qkv_bias.astype(
        jnp.float32
    )
    query = qkv[:, :breadth].reshape(row_count, heads, head_size)
    key_part = qkv[:, breadth : 2 * breadth].reshape(row_count, heads, head_size)
    value_part = qkv[:, 2 * breadth :].reshape(row_count, heads, head_size)
    query_feat, query_back = jax.vjp(lambda piece: feature_map(piece, projection), query)
    key_feat, key_back = jax.vjp(lambda piece: feature_map(piece, projection), key_part)
    query_low = to_low(query_feat).transpose(1, 0, 2)
    key_low = to_low(key_feat).transpose(1, 0, 2)
    value_low = to_low(value_part).transpose(1, 0, 2)
    coef_table = jnp.exp(full_rpe.astype(jnp.float32).reshape(heads, span))

    def forward_head(elements):
        return head_forward(elements[0], elements[1], elements[2], elements[3], segment, block_rows)

    context, denominator = lax.map(forward_head, (query_low, key_low, value_low, coef_table))
    context_low = to_low(context.transpose(1, 0, 2).reshape(row_count, breadth))
    attended = jnp.dot(
        context_low, full_out, preferred_element_type=jnp.float32
    ) + full_out_bias.astype(jnp.float32)
    normed, norm_one_back = jax.vjp(
        layer_norm,
        tokens.astype(jnp.float32) + attended,
        full_gain_one.astype(jnp.float32),
        full_bias_one.astype(jnp.float32),
    )
    normed_low = to_low(normed)
    upward = jnp.dot(normed_low, full_up, preferred_element_type=jnp.float32) + full_up_bias.astype(
        jnp.float32
    )
    activated, gelu_back = jax.vjp(exact_gelu, upward)
    activated_low = to_low(activated)
    downward = jnp.dot(
        activated_low, full_down, preferred_element_type=jnp.float32
    ) + full_down_bias.astype(jnp.float32)
    result, norm_two_back = jax.vjp(
        layer_norm,
        normed + downward,
        full_gain_two.astype(jnp.float32),
        full_bias_two.astype(jnp.float32),
    )
    back_qkv, back_out, back_up, back_down, back_rpe = (
        lax.all_gather(to_low(w_qkv), "dp", axis=0, tiled=True),
        lax.all_gather(to_low(w_out), "dp", axis=0, tiled=True),
        lax.all_gather(to_low(w_up), "dp", axis=0, tiled=True),
        lax.all_gather(to_low(w_down), "dp", axis=0, tiled=True),
        lax.all_gather(to_low(rpe_table), "dp", axis=0, tiled=True),
    )
    back_coef = jnp.exp(back_rpe.astype(jnp.float32).reshape(heads, span))
    grad_result = cotangent.astype(jnp.float32) * valid[:, None]
    grad_sum_two, grad_gain_two, grad_bias_two = norm_two_back(grad_result)
    grad_sum_low = to_low(grad_sum_two)
    grad_down = contract(activated_low, grad_sum_low, 0, 0)
    grad_down_bias = jnp.sum(grad_sum_two, axis=0)
    grad_active = contract(grad_sum_low, back_down, 1, 1)
    (grad_upward,) = gelu_back(grad_active)
    grad_up_low = to_low(grad_upward)
    grad_up = contract(normed_low, grad_up_low, 0, 0)
    grad_up_bias = jnp.sum(grad_upward, axis=0)
    grad_normed = contract(grad_up_low, back_up, 1, 1) + grad_sum_two
    grad_hidden, grad_gain_one, grad_bias_one = norm_one_back(grad_normed)
    grad_hidden_low = to_low(grad_hidden)
    grad_out_proj = contract(context_low, grad_hidden_low, 0, 0)
    grad_out_bias = jnp.sum(grad_hidden, axis=0)
    grad_context = (
        contract(grad_hidden_low, back_out, 1, 1)
        .reshape(row_count, heads, head_size)
        .transpose(1, 0, 2)
    )

    def backward_head(elements):
        return head_backward(
            elements[0],
            elements[1],
            elements[2],
            elements[3],
            segment,
            elements[4],
            elements[5],
            elements[6],
            block_rows,
        )

    grad_qfeat, grad_kfeat, grad_vals, grad_coef = lax.map(
        backward_head,
        (query_low, key_low, value_low, back_coef, context, denominator, grad_context),
    )
    (grad_query,) = query_back(grad_qfeat.transpose(1, 0, 2))
    (grad_keypart,) = key_back(grad_kfeat.transpose(1, 0, 2))
    grad_qkv = jnp.concatenate(
        [
            grad_query.reshape(row_count, breadth),
            grad_keypart.reshape(row_count, breadth),
            grad_vals.transpose(1, 0, 2).reshape(row_count, breadth),
        ],
        axis=1,
    )
    grad_qkv_low = to_low(grad_qkv)
    grad_qkv_weight = contract(tokens, grad_qkv_low, 0, 0)
    grad_qkv_bias = jnp.sum(grad_qkv, axis=0)
    grad_tokens = contract(grad_qkv_low, back_qkv, 1, 1) + grad_hidden
    grad_table = grad_coef.reshape(-1)
    shards = (
        lax.psum_scatter(grad_qkv_weight, "dp", scatter_dimension=0, tiled=True),
        lax.psum_scatter(grad_qkv_bias, "dp", scatter_dimension=0, tiled=True),
        lax.psum_scatter(grad_out_proj, "dp", scatter_dimension=0, tiled=True),
        lax.psum_scatter(grad_out_bias, "dp", scatter_dimension=0, tiled=True),
        lax.psum_scatter(grad_gain_one, "dp", scatter_dimension=0, tiled=True),
        lax.psum_scatter(grad_bias_one, "dp", scatter_dimension=0, tiled=True),
        lax.psum_scatter(grad_up, "dp", scatter_dimension=0, tiled=True),
        lax.psum_scatter(grad_up_bias, "dp", scatter_dimension=0, tiled=True),
        lax.psum_scatter(grad_down, "dp", scatter_dimension=0, tiled=True),
        lax.psum_scatter(grad_down_bias, "dp", scatter_dimension=0, tiled=True),
        lax.psum_scatter(grad_gain_two, "dp", scatter_dimension=0, tiled=True),
        lax.psum_scatter(grad_bias_two, "dp", scatter_dimension=0, tiled=True),
        lax.psum_scatter(grad_table, "dp", scatter_dimension=0, tiled=True),
    )
    return (
        to_low(result),
        grad_tokens,
        shards[0],
        shards[1],
        shards[2],
        shards[3],
        shards[4],
        shards[5],
        shards[6],
        shards[7],
        shards[8],
        shards[9],
        shards[10],
        shards[11],
        shards[12],
    )


def solution(mesh):
    in_specs = (
        P("dp", None),
        P("dp", None),
        P("dp", None),
        P(),
        P("dp", None),
        P("dp"),
        P("dp", None),
        P("dp"),
        P("dp"),
        P("dp"),
        P("dp", None),
        P("dp"),
        P("dp", None),
        P("dp"),
        P("dp"),
        P("dp"),
        P("dp"),
    )
    out_specs = (
        P("dp", None),
        P("dp", None),
        P("dp", None),
        P("dp"),
        P("dp", None),
        P("dp"),
        P("dp"),
        P("dp"),
        P("dp", None),
        P("dp"),
        P("dp", None),
        P("dp"),
        P("dp"),
        P("dp"),
        P("dp"),
    )
    return jax.shard_map(body, mesh=mesh, in_specs=in_specs, out_specs=out_specs, check_vma=False)
```

profile of v0, /device:TPU:0, one launch (start us, length us, event | category | flops | bytes accessed | tf_op | source)
XLA Modules:
  0.0 1401.4 jit_solution(3790954679005119528)
XLA Ops:
  16.1 42.5 %all-reduce.22 = (bf16[2304]{0:T(1024)(128)(2,1)S(1)}, bf16[768]{0:T(1024)(128)(2,1)S(1)}, bf16[768]{0:T(1024)(128)(2,1)S(1)}, bf16[768]{0:T(1024)(128)(2,1)S(1)...) all-reduce(bf16[2304]{0:T(1024)(128)(2,1)S(1)} %dynamic-update-slic, ...), channel_id=1, replica_groups=mesh['dp'=32] {'dp'}, use_global_device_ids=true, to_apply=%add.4 | all-reduce | flops 9984 | bytes 39936
  58.6 40.4 %all-gather = bf16[32,1,384]{2,1,0:T(2,128)(2,1)S(1)} all-gather(bf16[1,1,384]{2,1,0:T(2,128)(2,1)S(1)} %reshape.271), channel_id=1, replica_groups=mesh['dp'=32] {'dp'}, dimensions={0}, use_global_device_ids=true | all-gather | bytes 25344 | tf_op jit(solution)/shard_map/all_gather | solution.py:156
  101.2 4.0 convolution_add_fusion.1
  125.2 180.0 %while.33 = (s32[]{:T(128)}, f32[12,512,64]{1,2,0:T(8,128)}, f32[12,512]{1,0:T(8,128)}, bf16[12,512,64]{2,1,0:T(8,128)(2,1)}, bf16[12,512,64]{2,1,0:T(8,128)(2,1...) while((s32[]{:T(128)}, f32[12,512,64]{1,2,0:T(8,128)}, ...), condition=%wide.region_4.5_spmd.clone, body=%wide.region_2.4_spmd.clone.sunk | while | flops 68454400 | bytes 23629968 | solution.py:175
  313.7 19.9 %multiply_convert_fusion.1 = (bf16[512,3072]{1,0:T(8,128)(2,1)}, f32[512,3072]{1,0:T(8,128)}, f32[512,3072]{1,0:T(8,128)}) fusion(f32[3072]{0:T(1024)S(1)} %convert_element_type.187, bf16[768,3072]{1,0:T(8,128)(2,1)} %all-gather.10.cloned.1.call-done, f32[512,768]{1,0:T(8,128)S(1)} %get-tuple-element.543, f32[768]{0:T(1024)S(1)} %convert_element_type.183, ...), kind=kOutput, calls=%fused_computation.69 | convolution fusion | flops 2521694208 | bytes 22042624 | tf_op jit(solution)/shard_map/dot_general | solution.py:187
  333.6 6.0 fusion.109
  344.7 9.8 fusion.110
  354.6 5.6 multiply_reduce_fusion.1
  368.9 379.0 %while.34 = (s32[]{:T(128)}, f32[12,512,64]{1,2,0:T(8,128)}, f32[12,512,64]{1,2,0:T(8,128)}, f32[12,512,64]{1,2,0:T(8,128)}, f32[12,1024]{1,0:T(8,128)S(1)}, /*i...) while((s32[]{:T(128)}, f32[12,512,64]{1,2,0:T(8,128)}, ...), condition=%wide.region_16.17_spmd.clone, body=%wide.region_13.16_spmd.clone.sunk | while | flops 171117056 | bytes 46494936 | solution.py:243
  388.3 6.9 rev.41
  419.9 6.9 rev.41
  451.4 6.9 rev.41
  483.0 6.9 rev.41
  514.5 6.9 rev.41
  546.1 6.9 rev.41
  577.7 6.9 rev.41
  609.2 6.9 rev.41
  640.8 6.9 rev.41
  672.4 6.9 rev.41
  704.0 6.9 rev.41
  735.5 6.9 rev.41
  747.9 4.0 fusion.57
  762.7 6.9 convolution_bitcast_fusion.3
  769.6 8.1 copy.103
  779.1 7.3 fusion.66
  787.8 8.3 fusion.93
  797.5 6.2 convolution_add_fusion.2
  803.7 76.3 %all-reduce.25.cloned.1.call-done = (f32[2304]{0:T(1024)}, f32[768]{0:T(1024)}, f32[768]{0:T(1024)}, f32[768]{0:T(1024)}, f32[3072]{0:T(1024)}, /*index=5*/f32[7...) async-done(((f32[2304]{0:T(1024)}, f32[768]{0:T(1024)}, f32[768]{0:T(1024)}, f32[768]{0:T(1024)}, f32[3072]{0:T(1024)}, /*index=5*/f32[768]{0:T(1024)}, f32[768]{0:T(1024)}, ...) | async-done | bytes 89104
  891.4 95.1 %reduce-scatter.7.cloned.1.call-done = f32[24,768]{1,0:T(8,128)} async-done(((f32[768,768]{1,0:T(8,128)}), f32[24,768]{1,0:T(8,128)}) %reduce-scatter.7.cloned.1.call-update) | async-done | bytes 73744 | tf_op jit(solution)/shard_map/reduce_scatter | solution.py:265
  986.5 124.5 %reduce-scatter.13.cloned.1.call-done = f32[24,2304]{1,0:T(8,128)} async-done(((f32[768,2304]{1,0:T(8,128)}), f32[24,2304]{1,0:T(8,128)}) %reduce-scatter.13.cloned.1.call-update) | async-done | bytes 221200
  1111.0 142.3 %reduce-scatter.9.cloned.1.call-done = f32[24,3072]{1,0:T(8,128)} async-done(((f32[768,3072]{1,0:T(8,128)}), f32[24,3072]{1,0:T(8,128)}) %reduce-scatter.9.cloned.1.call-update) | async-done | bytes 294928 | tf_op jit(solution)/shard_map/reduce_scatter | solution.py:269
  1253.3 141.1 %reduce-scatter.11.cloned.1.call-done = f32[96,768]{1,0:T(8,128)} async-done(((f32[3072,768]{1,0:T(8,128)}), f32[96,768]{1,0:T(8,128)}) %reduce-scatter.11.cloned.1.call-update) | async-done | bytes 294928 | tf_op jit(solution)/shard_map/reduce_scatter | solution.py:271
  (755 shorter events, 552.5 us)
Async XLA Ops:
  7.2 104.2 %copy-start = (bf16[12,64,64]{2,1,0:T(8,128)(2,1)S(1)}, bf16[12,64,64]{2,1,0:T(8,128)(2,1)}, u32[]{:S(2)}) copy-start(bf16[12,64,64]{2,1,0:T(8,128)(2,1)} %param.26) | copy-start | bytes 294916
  7.2 7.0 copy-start.37
  7.2 7.0 copy-start.38
  7.2 7.0 copy-start.39
  7.2 7.0 copy-start.40
  7.2 7.0 copy-start.41
  7.2 7.1 copy-start.42
  7.3 7.1 copy-start.43
  7.3 7.1 copy-start.44
  7.3 51.3 %copy-start.31 = (f32[384]{0:T(512)S(1)}, f32[384]{0:T(512)}, u32[]{:S(2)}) copy-start(f32[384]{0:T(512)} %param.39) | copy-start | bytes 4612
  7.3 92.0 %copy-start.32 = (s32[1,2]{1,0:T(1,128)S(1)}, s32[1,2]{1,0:T(1,128)}, u32[]{:S(2)}) copy-start(s32[1,2]{1,0:T(1,128)} %param.25) | copy-start | bytes 28
  7.3 93.9 %copy-start.35 = (bf16[512,768]{1,0:T(8,128)(2,1)S(1)}, bf16[512,768]{1,0:T(8,128)(2,1)}, u32[]{:S(2)}) copy-start(bf16[512,768]{1,0:T(8,128)(2,1)} %param.23) | copy-start | bytes 2359300
  7.3 93.9 %all-gather.6.cloned.1.call-start = ((), (), s32[]{:S(2)}) async-start(), calls=%async_computation.4 | async-start | bytes 3649536 | tf_op jit(solution)/shard_map/all_gather | solution.py:144
  9.1 302.0 %all-gather.8.cloned.1.call-start = ((), (), s32[]{:S(2)}) async-start(), calls=%async_computation.5 | async-start | bytes 1216512 | tf_op jit(solution)/shard_map/all_gather | solution.py:146
  10.7 303.0 %all-gather.10.cloned.1.call-start = ((), (), s32[]{:S(2)}) async-start(), calls=%async_computation.6 | async-start | bytes 4866048 | tf_op jit(solution)/shard_map/all_gather | solution.py:150
  12.4 321.2 %all-gather.12.cloned.1.call-start = ((), (), s32[]{:S(2)}) async-start(), calls=%async_computation.7 | async-start | bytes 4866048 | tf_op jit(solution)/shard_map/all_gather | solution.py:152
  14.1 865.9 %all-reduce.25.cloned.1.call-start = ((), (), s32[]{:S(2)}) async-start(), calls=%async_computation.12 | async-start | bytes 196608
  99.8 233.8 %copy-start.29 = (f32[768]{0:T(1024)}, f32[768]{0:T(1024)S(1)}, u32[]{:S(2)}) copy-start(f32[768]{0:T(1024)S(1)} %convert_element_type.183) | copy-start | bytes 9220
  313.3 46.9 %copy-start.9 = (f32[512,768]{1,0:T(8,128)}, f32[512,768]{1,0:T(8,128)S(1)}, u32[]{:S(2)}) copy-start(f32[512,768]{1,0:T(8,128)S(1)} %get-tuple-element.543) | copy-start | bytes 4718596
  342.1 12.5 slice-start.1
  343.9 10.7 copy-start.11
  343.9 10.7 copy-start.27
  344.7 9.9 slice-start.2
  368.9 379.0 %copy-start.25 = (f32[512,12]{0,1:T(8,128)S(1)}, f32[512,12]{0,1:T(8,128)}, u32[]{:S(2)}) copy-start(f32[512,12]{0,1:T(8,128)} %get-tuple-element.532) | copy-start | bytes 73732
  368.9 379.0 %copy-start.26 = (f32[512,12]{0,1:T(8,128)S(1)}, f32[512,12]{0,1:T(8,128)}, u32[]{:S(2)}) copy-start(f32[512,12]{0,1:T(8,128)} %get-tuple-element.534) | copy-start | bytes 73732
  747.9 4.6 copy-start.4
  747.9 4.6 copy-start.6
  747.9 4.6 copy-start.24
  758.5 228.0 %reduce-scatter.7.cloned.1.call-start = ((), (), s32[]{:S(2)}) async-start(), calls=%async_computation.8 | async-start | bytes 2433024 | tf_op jit(solution)/shard_map/reduce_scatter | solution.py:265
  762.4 348.6 %reduce-scatter.13.cloned.1.call-start = ((), (), s32[]{:S(2)}) async-start(), calls=%async_computation.11 | async-start | bytes 7299072
  777.7 475.6 %reduce-scatter.9.cloned.1.call-start = ((), (), s32[]{:S(2)}) async-start(), calls=%async_computation.9 | async-start | bytes 9732096 | tf_op jit(solution)/shard_map/reduce_scatter | solution.py:269
  786.5 607.9 %reduce-scatter.11.cloned.1.call-start = ((), (), s32[]{:S(2)}) async-start(), calls=%async_computation.10 | async-start | bytes 9732096 | tf_op jit(solution)/shard_map/reduce_scatter | solution.py:271
  (36 other events, 63.5 us)
Sparse Core Ops, SparseCore 0:
  11.6 62.9 all-gather.5
  78.1 52.8 all-gather.7
  134.4 62.5 all-gather.9
  200.4 62.7 all-gather.11
  758.6 121.3 all-reduce.24
  886.5 99.9 reduce-scatter.6
  992.8 118.1 reduce-scatter.12
  1118.5 134.7 reduce-scatter.8
  1259.8 134.5 reduce-scatter.10
where the time goes:
time: 1420 us; the launch traced here: 1400 us
  waiting for transfers between devices  579 us (41%)
  local copies, waits for them, and re-layouts  447 us (31%)
  matrix products  228 us (16%)
  blocking collectives  82.9 us (6%)
  other arithmetic  44.8 us (3%)
  between operations  16.3 us (1%)
    unnamed x11, waiting for transfers between devices  201 us
    dot_general x68, matrix products, contract(): lax.dot_general(first_op, second_op, (((first_dim,), (second_dim,)), ((),...  143 us
    reduce_scatter x1, waiting for transfers between devices, body(): lax.psum_scatter(grad_up, 'dp', scatter_dimension=0, tiled=True)  142 us
    reduce_scatter x1, waiting for transfers between devices, body(): lax.psum_scatter(grad_down, 'dp', scatter_dimension=0, tiled=True)  141 us
    reduce_scatter x1, waiting for transfers between devices, body(): lax.psum_scatter(grad_out_proj, 'dp', scatter_dimension=0, tiled=True)  95.1 us
    rev x12, local copies, waits for them, and re-layouts, diagonal_sums(): matrix[::-1]  82.2 us
    reshape x24, local copies, waits for them, and re-layouts, toeplitz_block(): jnp.broadcast_to(vector[::-1], (height, height + breadth - 1)).reshape(-1)  66.7 us
    unnamed x1, blocking collectives  42.5 us
  transfers between devices with their start and end apart: 9, of which 5 were waited for; matrix products, arithmetic and copies ran while one was open for 21% of the time, Pallas kernels for 0%

commit v1 on v0

v1 whole, which is shorter than its diff:
```python
import functools

import jax
import jax.numpy as jnp
from jax import lax
from jax.experimental import pallas as pl
from jax.experimental.pallas import tpu as pltpu
from jax.sharding import PartitionSpec as P

EPSILON = 1e-05
F32 = jnp.float32
LOW = jnp.bfloat16
MESH = pl.DeviceIdType.MESH
MIB = 2**20


def mm(first_op, second_op, first_dim=1, second_dim=0):
    return lax.dot_general(
        first_op,
        second_op,
        (((first_dim,), (second_dim,)), ((), ())),
        preferred_element_type=F32,
    )


def mm2(value, weight, weight_dim=0):
    high = value.astype(LOW)
    rest = (value - high.astype(F32)).astype(LOW)
    return mm(high, weight, 1, weight_dim) + mm(rest, weight, 1, weight_dim)


def iota(shape, dim):
    return lax.broadcasted_iota(jnp.int32, shape, dim)


def cols(index, width):
    return pl.ds(pl.multiple_of(index * width, width), width)


def build_tables(seq_ref, feat_ref, mask_ref, block_ref, ones_ref):
    rows = mask_ref.shape[0]
    first_end = seq_ref[0, 0]
    second_end = first_end + seq_ref[0, 1]

    def segment(place):
        return (place >= first_end).astype(jnp.int32) + (place >= second_end).astype(jnp.int32)

    across = segment(iota((128, rows), 1))
    for start in range(0, rows, 128):
        down = segment(iota((128, rows), 0) + start)
        mask_ref[start : start + 128, :] = jnp.where(down == across, 1.0, 0.0)
    head_size = feat_ref.shape[1]
    breadth = ones_ref.shape[0]
    group = breadth // head_size
    bits = head_size.bit_length() - 1
    owner_row = lax.shift_right_logical(iota((breadth, breadth), 0), bits)
    owner_col = lax.shift_right_logical(iota((breadth, breadth), 1), bits)
    same = owner_row == owner_col
    ones_ref[...] = jnp.where(same, 1.0, 0.0).astype(LOW)
    for index in range(feat_ref.shape[0] // group):
        rows_of = []
        for inner in range(group):
            piece = feat_ref[index * group + inner].astype(F32)
            rows_of.append(jnp.concatenate([piece] * group, axis=1))
        full = jnp.concatenate(rows_of, axis=0)
        block_ref[index] = jnp.where(same, full, 0.0).astype(LOW)


def project(tokens_ref, w_ref, vec_ref, scaled_ref, phi_ref, low_ref, block_ref, ones_ref):
    breadth = tokens_ref.shape[1]
    tile = ones_ref.shape[0]
    per_part = breadth // tile
    scale = 64 ** (-0.25)

    def features(step, carry):
        where = cols(step, tile)
        acc = mm(tokens_ref[...], w_ref[:, where]) + vec_ref[0:1, where]
        scaled = acc * scale
        scaled_ref[:, where] = scaled
        block = block_ref[lax.rem(step, per_part)]
        mapped = mm2(scaled, block)
        squared = mm2(scaled * scaled, ones_ref[...])
        phi = jnp.exp(mapped - 0.5 * squared) * 0.125
        phi_ref[:, where] = phi
        low_ref[:, where] = phi.astype(LOW)
        return carry

    lax.fori_loop(0, 2 * per_part, features, 0)

    def plain(step, carry):
        where = cols(step + 2 * per_part, tile)
        acc = mm(tokens_ref[...], w_ref[:, where]) + vec_ref[0:1, where]
        low_ref[:, where] = acc.astype(LOW)
        return carry

    lax.fori_loop(0, per_part, plain, 0)


def coefficients(rpe_ref, head, coef_ref):
    flip = (iota((128, 128), 0) + iota((128, 128), 1) == 127).astype(F32).astype(LOW)
    raw = rpe_ref[pl.ds(pl.multiple_of(head * 8, 8), 8), :].astype(LOW)
    table = jnp.exp(mm(raw, flip))
    wide = jnp.concatenate(
        [jnp.broadcast_to(table[7 - k : 8 - k, :], (128, 128)) for k in range(8)], axis=1
    )
    coef_ref[...] = pltpu.roll(wide, 1024 - 127, axis=1, stride=1, stride_axis=0)


def attend(low_ref, rpe_ref, mask_ref, den_ref, ctx_ref, ctx_low_ref, coef_ref, key_ref):
    rows, breadth = ctx_ref.shape

    def pair_step(pair, carry):
        q_at = cols(pair, 128)
        k_at = pl.ds(pl.multiple_of(pair * 128 + breadth, 128), 128)
        v_at = pl.ds(pl.multiple_of(pair * 128 + 2 * breadth, 128), 128)
        lane = iota((128, 128), 1)
        for side in range(2):
            coefficients(rpe_ref, pair * 2 + side, coef_ref)
            mine = lane >= 64 if side else lane < 64
            keep_half(low_ref, k_at, key_ref, side)
            for block in range(rows // 128):
                at = slice(block * 128, block * 128 + 128)
                kernel = mm(low_ref[at, q_at], key_ref[...], 1, 1)
                lead = 128 * (rows // 128 - 1 - block)
                scores = kernel * (coef_ref[:, lead : lead + rows] * mask_ref[at, :])
                total = jnp.sum(scores, axis=1, keepdims=True)
                context = mm(scores.astype(LOW), low_ref[:, v_at]) * (1.0 / total)
                total = jnp.broadcast_to(total, (128, 128))
                if side == 0:
                    den_ref[at, q_at] = total
                    ctx_ref[at, q_at] = context
                else:
                    den_ref[at, q_at] = jnp.where(mine, total, den_ref[at, q_at])
                    context = jnp.where(mine, context, ctx_ref[at, q_at])
                    ctx_ref[at, q_at] = context
                    ctx_low_ref[at, q_at] = context.astype(LOW)
        return carry

    lax.fori_loop(0, breadth // 128, pair_step, 0)


def keep_half(low_ref, where, out_ref, side):
    rows = low_ref.shape[0]
    lane = iota((rows, 128), 1)
    mine = lane >= 64 if side else lane < 64
    out_ref[...] = jnp.where(mine, low_ref[:, where].astype(F32), 0.0).astype(LOW)


def forward_kernel(
    seq_ref, tokens_ref, feat_ref, w_ref, vec_ref, rpe_ref,
    scaled_ref, phi_ref, low_ref, den_ref, ctx_ref, ctx_low_ref,
    mask_ref, block_ref, ones_ref, coef_ref, key_ref,
):
    build_tables(seq_ref, feat_ref, mask_ref, block_ref, ones_ref)
    project(tokens_ref, w_ref, vec_ref, scaled_ref, phi_ref, low_ref, block_ref, ones_ref)
    attend(low_ref, rpe_ref, mask_ref, den_ref, ctx_ref, ctx_low_ref, coef_ref, key_ref)


def norm(value):
    centred = value - jnp.mean(value, axis=-1, keepdims=True)
    inverse = lax.rsqrt(jnp.mean(centred * centred, axis=-1, keepdims=True) + EPSILON)
    return centred * inverse, inverse


def norm_back(grad, xhat, inverse, gain):
    scaled = grad * gain
    mean = jnp.mean(scaled, axis=-1, keepdims=True)
    along = jnp.mean(scaled * xhat, axis=-1, keepdims=True)
    return inverse * (scaled - mean - xhat * along)


def add_to(ref, row, value):
    ref[row : row + 1, 0 : value.shape[1]] += value


def column_sum(value):
    return jnp.sum(value, axis=0, keepdims=True)


def middle_kernel(
    seq_ref, tokens_ref, cot_ref, ctx_low_ref, vec_ref, w_out_ref, w_up_ref, w_down_ref,
    out_ref, g_hidden_ref, g_ctx_ref, d_out_ref, d_up_ref, d_down_ref, gvec_ref,
    wide_ref, normed_ref, normed_low_ref, xhat_ref, inverse_ref, act_ref, slope_ref, g_sum_ref,
    g_low_ref, g_up_ref, flip_ref,
):
    rows, breadth = tokens_ref.shape
    hidden = w_up_ref.shape[1]
    height, tile = 128, 256
    blocks, tiles = rows // height, breadth // tile
    valid_rows = seq_ref[0, 0] + seq_ref[0, 1]
    gvec_ref[...] = jnp.zeros_like(gvec_ref)
    gain_one, bias_one = vec_ref[3:4, :breadth], vec_ref[4:5, :breadth]
    gain_two, bias_two = vec_ref[6:7, :breadth], vec_ref[7:8, :breadth]

    def rows_at(step):
        return pl.ds(pl.multiple_of(step * height, height), height)

    def loop(count, step):
        def run(index, carry):
            step(index)
            return carry

        lax.fori_loop(0, count, run, 0)

    def attended_step(step):
        where = cols(step, tile)
        wide_ref[:, where] = mm(ctx_low_ref[...], w_out_ref[:, where]) + vec_ref[2:3, where]

    loop(tiles, attended_step)

    def first_norm(step):
        at = rows_at(step)
        xhat, inverse = norm(tokens_ref[at, :].astype(F32) + wide_ref[at, :])
        xhat_ref[at, :] = xhat
        inverse_ref[at, :] = jnp.broadcast_to(inverse, (height, 128))
        normed = xhat * gain_one + bias_one
        normed_ref[at, :] = normed
        normed_low_ref[at, :] = normed.astype(LOW)

    loop(blocks, first_norm)

    def upward_step(step):
        where = cols(step, tile)
        upward = mm(normed_low_ref[...], w_up_ref[:, where]) + vec_ref[1:2, where]
        phi = 0.5 + 0.5 * lax.erf(upward * 0.5**0.5)
        density = jnp.exp(-0.5 * upward * upward) * 0.3989422804014327
        act_ref[:, where] = (upward * phi).astype(LOW)
        slope_ref[:, where] = phi + upward * density

    loop(hidden // tile, upward_step)

    def downward_step(step):
        where = cols(step, tile)
        wide_ref[:, where] = mm(act_ref[...], w_down_ref[:, where]) + vec_ref[5:6, where]

    loop(tiles, downward_step)

    def second_norm(step):
        at = rows_at(step)
        xhat, inverse = norm(normed_ref[at, :] + wide_ref[at, :])
        out_ref[at, :] = (xhat * gain_two + bias_two).astype(LOW)
        place = iota((height, breadth), 0) + step * height
        grad = jnp.where(place < valid_rows, cot_ref[at, :].astype(F32), 0.0)
        add_to(gvec_ref, 6, column_sum(grad * xhat))
        add_to(gvec_ref, 7, column_sum(grad))
        g_sum = norm_back(grad, xhat, inverse, gain_two)
        add_to(gvec_ref, 5, column_sum(g_sum))
        g_sum_ref[at, :] = g_sum
        g_low_ref[at, :] = g_sum.astype(LOW)

    loop(blocks, second_norm)
    flip_ref[...] = jnp.transpose(normed_low_ref[...])

    def down_step(step):
        where = cols(step, tile)
        g_upward = mm(g_low_ref[...], w_down_ref[where, :], 1, 1) * slope_ref[:, where]
        gvec_ref[1:2, where] = column_sum(g_upward)
        g_upward = g_upward.astype(LOW)
        g_up_ref[:, where] = g_upward
        d_down_ref[where, :] = mm(act_ref[:, where], g_low_ref[...], 0, 0).astype(LOW)
        d_up_ref[:, where] = mm(flip_ref[...], g_upward).astype(LOW)

    loop(hidden // tile, down_step)

    def up_back(step):
        where = cols(step, tile)
        wide_ref[:, where] = mm(g_up_ref[...], w_up_ref[where, :], 1, 1) + g_sum_ref[:, where]

    loop(tiles, up_back)

    def first_back(step):
        at = rows_at(step)
        g_normed = wide_ref[at, :]
        xhat = xhat_ref[at, :]
        add_to(gvec_ref, 3, column_sum(g_normed * xhat))
        add_to(gvec_ref, 4, column_sum(g_normed))
        g_hidden = norm_back(g_normed, xhat, inverse_ref[at, 0:1], gain_one)
        add_to(gvec_ref, 2, column_sum(g_hidden))
        g_hidden_ref[at, :] = g_hidden
        g_low_ref[at, :] = g_hidden.astype(LOW)

    loop(blocks, first_back)

    def out_back(step):
        where = cols(step, tile)
        g_ctx_ref[:, where] = mm(g_low_ref[...], w_out_ref[where, :], 1, 1)
        d_out_ref[where, :] = mm(ctx_low_ref[:, where], g_low_ref[...], 0, 0).astype(LOW)

    loop(tiles, out_back)


def diagonals(diag_ref, out_ref, head):
    value = diag_ref[...]
    height = value.shape[0]
    while height > 1:
        height //= 2
        value = value[height:] + pltpu.roll(value[:height], height, axis=1)
    for k in range(8):
        out_ref[pl.ds(head * 8 + 7 - k, 1), :] = value[:, 128 * k : 128 * k + 128]


def attend_back(
    low_ref, rpe_ref, mask_ref, den_ref, ctx_ref, g_ctx_ref,
    g_feat_ref, g_low_ref, gvec_ref, grpe_ref,
    coef_ref, scores_ref, gk_ref, diag_ref, query_ref, key_ref, value_ref, num_ref,
):
    rows, breadth = ctx_ref.shape

    def pair_step(pair, carry):
        q_at = cols(pair, 128)
        k_at = pl.ds(pl.multiple_of(pair * 128 + breadth, 128), 128)
        v_at = pl.ds(pl.multiple_of(pair * 128 + 2 * breadth, 128), 128)
        lane = iota((128, 128), 1)
        ones = jnp.ones((128, 128), LOW)
        for side in range(2):
            coefficients(rpe_ref, pair * 2 + side, coef_ref)
            mine = lane >= 64 if side else lane < 64
            other = 0 if side else 64
            keep_half(low_ref, q_at, query_ref, side)
            keep_half(low_ref, k_at, key_ref, side)
            keep_half(low_ref, v_at, value_ref, side)
            diag_ref[...] = jnp.zeros_like(diag_ref)
            is_high, is_rest = lane == other, lane == other + 1
            extra = jnp.where(jnp.logical_or(is_high, is_rest), 1.0, 0.0)
            for block in range(rows // 128):
                at = slice(block * 128, block * 128 + 128)
                value_ref[at, :] = (value_ref[at, :].astype(F32) + extra).astype(LOW)
            for block in range(rows // 128):
                at = slice(block * 128, block * 128 + 128)
                kernel = mm(low_ref[at, q_at], key_ref[...], 1, 1)
                g_num = jnp.where(mine, g_ctx_ref[at, q_at] * (1.0 / den_ref[at, q_at]), 0.0)
                g_den = -mm2(g_num * ctx_ref[at, q_at], ones)
                num_ref[at, :] = g_num.astype(LOW)
                high = g_den.astype(LOW).astype(F32)
                extended = jnp.where(is_high, high, jnp.where(is_rest, g_den - high, g_num))
                g_scores = mm(extended.astype(LOW), value_ref[...], 1, 1)
                lead = 128 * (rows // 128 - 1 - block)
                weight = coef_ref[:, lead : lead + rows] * mask_ref[at, :]
                scores = kernel * weight
                g_kernel = (g_scores * weight).astype(LOW)
                diag_ref[:, lead : lead + rows] += g_scores * scores
                scores_ref[at, :] = scores.astype(LOW)
                gk_ref[at, :] = g_kernel
                g_query = mm(g_kernel, key_ref[...])
                if side:
                    g_query = g_query + g_feat_ref[at, q_at]
                g_feat_ref[at, q_at] = g_query
            g_key = mm(gk_ref[...], query_ref[...], 0, 0)
            g_value = mm(scores_ref[...], num_ref[...], 0, 0)
            if side:
                g_key = g_key + g_feat_ref[:, k_at]
                g_value = g_value + g_feat_ref[:, v_at]
            g_feat_ref[:, k_at] = g_key
            g_feat_ref[:, v_at] = g_value
            diagonals(diag_ref, grpe_ref, pair * 2 + side)
        g_value = g_feat_ref[:, v_at]
        gvec_ref[0:1, v_at] = column_sum(g_value)
        g_low_ref[:, v_at] = g_value.astype(LOW)
        return carry

    lax.fori_loop(0, breadth // 128, pair_step, 0)
    flip = (jnp.where(iota((128, 128), 0) + iota((128, 128), 1) == 127, 1.0, 0.0)).astype(LOW)
    grpe_ref[...] = mm2(grpe_ref[...], flip)


def project_back(
    tokens_ref, w_ref, g_hidden_ref, phi_ref, scaled_ref, block_ref, ones_ref,
    g_feat_ref, g_low_ref, gvec_ref, g_tokens_ref, d_qkv_ref, flip_ref,
):
    breadth = tokens_ref.shape[1]
    tile = ones_ref.shape[0]
    per_part = breadth // tile
    scale = 64 ** (-0.25)

    def features(step, carry):
        where = cols(step, tile)
        upward = g_feat_ref[:, where] * phi_ref[:, where]
        total = mm2(upward, ones_ref[...])
        grad = mm2(upward, block_ref[lax.rem(step, per_part)], 1) - scaled_ref[:, where] * total
        grad = grad * scale
        gvec_ref[0:1, where] = column_sum(grad)
        g_low_ref[:, where] = grad.astype(LOW)
        return carry

    lax.fori_loop(0, 2 * per_part, features, 0)
    flip_ref[...] = jnp.transpose(tokens_ref[...])

    def weights(step, carry):
        where = cols(step, tile)
        d_qkv_ref[:, where] = mm(flip_ref[...], g_low_ref[:, where]).astype(LOW)
        return carry

    lax.fori_loop(0, 3 * per_part, weights, 0)

    def inputs(step, carry):
        where = cols(step, tile)
        g_tokens_ref[:, where] = mm(g_low_ref[...], w_ref[where, :], 1, 1) + g_hidden_ref[:, where]
        return carry

    lax.fori_loop(0, per_part, inputs, 0)


def backward_kernel(
    seq_ref, tokens_ref, feat_ref, w_ref, rpe_ref, scaled_ref, phi_ref, low_ref, den_ref, ctx_ref,
    g_ctx_ref, g_hidden_ref,
    g_tokens_ref, d_qkv_ref, gvec_ref, grpe_ref,
    mask_ref, block_ref, ones_ref, coef_ref, g_feat_ref, g_low_ref, scores_ref, gk_ref, diag_ref,
    query_ref, key_ref, value_ref, num_ref, flip_ref,
):
    build_tables(seq_ref, feat_ref, mask_ref, block_ref, ones_ref)
    gvec_ref[...] = jnp.zeros_like(gvec_ref)
    attend_back(
        low_ref, rpe_ref, mask_ref, den_ref, ctx_ref, g_ctx_ref, g_feat_ref, g_low_ref, gvec_ref, grpe_ref,
        coef_ref, scores_ref, gk_ref, diag_ref, query_ref, key_ref, value_ref, num_ref,
    )
    project_back(
        tokens_ref, w_ref, g_hidden_ref, phi_ref, scaled_ref, block_ref, ones_ref,
        g_feat_ref, g_low_ref, gvec_ref, g_tokens_ref, d_qkv_ref, flip_ref,
    )


def vmem(count):
    return [pl.BlockSpec(memory_space=pltpu.VMEM)] * count


def shape(dims, kind):
    return jax.ShapeDtypeStruct(dims, kind)


SCALARS = pl.BlockSpec(memory_space=pltpu.SMEM)


def forward_call(seq, tokens, feat, w_qkv, vec, rpe):
    rows, breadth = tokens.shape
    span = 2 * rows
    return pl.pallas_call(
        forward_kernel,
        out_shape=(
            shape((rows, 2 * breadth), F32), shape((rows, 2 * breadth), F32), shape((rows, 3 * breadth), LOW),
            shape((rows, breadth), F32), shape((rows, breadth), F32), shape((rows, breadth), LOW),
        ),
        in_specs=[SCALARS] + vmem(5),
        out_specs=tuple(vmem(6)),
        scratch_shapes=[
            pltpu.VMEM((rows, rows), F32), pltpu.VMEM((breadth // 256, 256, 256), LOW),
            pltpu.VMEM((256, 256), LOW), pltpu.VMEM((128, span), F32), pltpu.VMEM((rows, 128), LOW),
        ],
        compiler_params=pltpu.CompilerParams(vmem_limit_bytes=60 * MIB),
        name="attend",
    )(seq, tokens, feat, w_qkv, vec, rpe)


def middle_call(seq, tokens, cotangent, ctx_low, vec, w_out, w_up, w_down):
    rows, breadth = tokens.shape
    hidden = w_up.shape[1]
    return pl.pallas_call(
        middle_kernel,
        out_shape=(
            shape((rows, breadth), LOW), shape((rows, breadth), F32), shape((rows, breadth), F32),
            shape(w_out.shape, LOW), shape(w_up.shape, LOW), shape(w_down.shape, LOW), shape(vec.shape, F32),
        ),
        in_specs=[SCALARS] + vmem(7),
        out_specs=tuple(vmem(7)),
        scratch_shapes=[
            pltpu.VMEM((rows, breadth), F32), pltpu.VMEM((rows, breadth), F32), pltpu.VMEM((rows, breadth), LOW),
            pltpu.VMEM((rows, breadth), F32), pltpu.VMEM((rows, 128), F32), pltpu.VMEM((rows, hidden), LOW),
            pltpu.VMEM((rows, hidden), F32), pltpu.VMEM((rows, breadth), F32), pltpu.VMEM((rows, breadth), LOW),
            pltpu.VMEM((rows, hidden), LOW), pltpu.VMEM((breadth, rows), LOW),
        ],
        compiler_params=pltpu.CompilerParams(vmem_limit_bytes=60 * MIB),
        name="feed_forward",
    )(seq, tokens, cotangent, ctx_low, vec, w_out, w_up, w_down)


def backward_call(seq, tokens, feat, w_qkv, rpe, scaled, phi, low, den, ctx, g_ctx, g_hidden, vec):
    rows, breadth = tokens.shape
    span = 2 * rows
    return pl.pallas_call(
        backward_kernel,
        out_shape=(
            shape((rows, breadth), F32), shape(w_qkv.shape, LOW), shape(vec.shape, F32), shape(rpe.shape, F32),
        ),
        in_specs=[SCALARS] + vmem(11),
        out_specs=tuple(vmem(4)),
        scratch_shapes=[
            pltpu.VMEM((rows, rows), F32), pltpu.VMEM((breadth // 256, 256, 256), LOW),
            pltpu.VMEM((256, 256), LOW), pltpu.VMEM((128, span), F32), pltpu.VMEM((rows, 3 * breadth), F32),
            pltpu.VMEM((rows, 3 * breadth), LOW), pltpu.VMEM((rows, rows), LOW), pltpu.VMEM((rows, rows), LOW),
            pltpu.VMEM((128, span), F32), pltpu.VMEM((rows, 128), LOW), pltpu.VMEM((rows, 128), LOW),
            pltpu.VMEM((rows, 128), LOW), pltpu.VMEM((rows, 128), LOW), pltpu.VMEM((breadth, rows), LOW),
        ],
        compiler_params=pltpu.CompilerParams(vmem_limit_bytes=60 * MIB),
        name="attend_back",
    )(seq, tokens, feat, w_qkv, rpe, scaled, phi, low, den, ctx, g_ctx, g_hidden)


PIECE = 16


def place():
    me = lax.axis_index("dp")
    core = lax.rem(me, 2)
    x = lax.rem(me // 2, 2)
    y = lax.rem(me // 4, 2)
    z = me // 8
    first = x * (1 - core) + y * core
    second = y * (1 - core) + x * core
    return core, z, first, second


class Plane:
    def __init__(self, depth):
        self.depth = depth
        self.core, self.z, self.first, self.second = place()
        self.chip = self.at(self.z, self.first, self.second)
        self.sibling = self.chip * 2 + 1 - self.core
        self.over_first = self.device(self.z, 1 - self.first, self.second)
        self.over_second = self.device(self.z, self.first, 1 - self.second)

    def at(self, z, first, second):
        return 4 * z + first * (1 + self.core) + second * (2 - self.core)

    def device(self, z, first, second):
        return 2 * self.at(z, first, second) + self.core

    def ahead(self, distance):
        return lax.rem(self.z + distance, self.depth)

    def behind(self, distance):
        return lax.rem(self.z + self.depth - distance, self.depth)

    def greet(self):
        barrier = pltpu.get_barrier_semaphore()
        others = [self.sibling, self.over_first, self.over_second]
        others += [self.device(self.ahead(d), self.first, self.second) for d in range(1, self.depth)]
        for other in others:
            pl.semaphore_signal(barrier, inc=1, device_id=(other,), device_id_type=MESH)
        pl.semaphore_wait(barrier, len(others))


def remote(source, target, sems, item, slot, device):
    return pltpu.make_async_remote_copy(
        src_ref=source, dst_ref=target, send_sem=sems[0].at[item, slot], recv_sem=sems[1].at[item, slot],
        device_id=(device,), device_id_type=MESH,
    )


def each(count, step):
    def run(index, carry):
        step(index)
        return carry

    lax.fori_loop(0, count, run, 0)


class Gather:
    def __init__(self, plane, own, full, sems, local):
        self.plane, self.own, self.full, self.sems, self.local = plane, own, full, sems, local
        depth = plane.depth
        self.first_slot = depth - 1
        self.second_slot = self.first_slot + depth
        self.core_slot = self.second_slot + 2 * depth
        self.slots = self.core_slot + 4 * depth

    def block(self, item, chip):
        return self.full[item].at[chip, self.plane.core]

    def to_first(self, item, z, source=None):
        block = self.block(item, self.plane.at(z, self.plane.first, self.plane.second))
        return remote(block if source is None else source, block, self.sems, item, self.first_slot + z, self.plane.over_first)

    def to_second(self, item, z, first, source=None):
        block = self.block(item, self.plane.at(z, first, self.plane.second))
        return remote(
            block if source is None else source, block, self.sems, item, self.second_slot + 2 * z + first, self.plane.over_second
        )

    def to_core(self, item, chip, source=None):
        block = self.block(item, chip)
        return remote(block if source is None else source, block, self.sems, item, self.core_slot + chip, self.plane.sibling)

    def to_depth(self, item, distance):
        plane = self.plane
        target = plane.device(plane.ahead(distance), plane.first, plane.second)
        return remote(self.own[item], self.block(item, plane.chip), self.sems, item, distance - 1, target)

    def copy_own(self, item):
        return pltpu.make_async_copy(self.own[item], self.block(item, self.plane.chip), self.local.at[item])

    def begin(self, item):
        plane = self.plane
        own = self.own[item]
        for distance in range(1, plane.depth):
            self.to_depth(item, distance).start()
        self.to_first(item, plane.z, own).start()
        self.to_second(item, plane.z, plane.first, own).start()
        self.to_core(item, plane.chip, own).start()
        self.copy_own(item).start()

    def arrived(self, copy):
        copy.wait_recv()

    def over_depth(self, item):
        plane = self.plane

        def step(index):
            z = plane.behind(index + 1)
            chip = plane.at(z, plane.first, plane.second)
            block = self.block(item, chip)
            remote(block, block, self.sems, item, index, plane.over_first).wait_recv()
            self.to_first(item, z).start()
            self.to_second(item, z, plane.first).start()
            self.to_core(item, chip).start()

        each(plane.depth - 1, step)

    def over_first(self, item):
        plane = self.plane

        def step(z):
            chip = plane.at(z, 1 - plane.first, plane.second)
            block = self.block(item, chip)
            remote(block, block, self.sems, item, self.first_slot + z, plane.over_first).wait_recv()
            self.to_second(item, z, 1 - plane.first).start()
            self.to_core(item, chip).start()

        each(plane.depth, step)

    def over_second(self, item):
        plane = self.plane

        def step(index):
            z, first = index // 2, lax.rem(index, 2)
            chip = plane.at(z, first, 1 - plane.second)
            block = self.block(item, chip)
            remote(block, block, self.sems, item, self.second_slot + index, plane.over_second).wait_recv()
            self.to_core(item, chip).start()

        each(2 * plane.depth, step)

    def over_core(self, item):
        plane = self.plane

        def step(chip):
            block = self.full[item].at[chip, 1 - plane.core]
            remote(block, block, self.sems, item, self.core_slot + chip, plane.sibling).wait_recv()

        each(4 * plane.depth, step)
        self.copy_own(item).wait()

    def sent(self, item):
        plane = self.plane
        block = self.block(item, plane.chip)

        def step(slot):
            remote(block, block, self.sems, item, slot, plane.sibling).wait_send()

        each(self.slots, step)


def one_hot(length, breadth):
    factor = (1 << 20) // length + 1
    col = iota((128, breadth), 1)
    owner = lax.shift_right_logical(col * factor, 20)
    return jnp.where(iota((128, breadth), 0) == col - owner * length, 1.0, 0.0).astype(LOW)


def owned(devices, length, breadth):
    factor = (1 << 20) // length + 1
    col = iota((devices, breadth), 1)
    return lax.shift_right_logical(col * factor, 20) == iota((devices, breadth), 0)


def pack_small(piece_refs, small_ref):
    small_ref[...] = jnp.zeros_like(small_ref)
    for row, piece in enumerate(piece_refs[:-1]):
        small_ref[row : row + 1, 0 : piece.shape[1]] = piece[...].astype(LOW).astype(F32)
    table = piece_refs[-1]
    for part in range(table.shape[1] // 128):
        row = len(piece_refs) - 1 + part
        small_ref[row : row + 1, :] = table[:, 128 * part : 128 * part + 128].astype(LOW).astype(F32)


def unpack_small(all_ref, lengths, table_rows, vec_ref, rpe_ref):
    devices = all_ref.shape[0] // PIECE
    vec_ref[...] = jnp.zeros_like(vec_ref)
    for row, length in enumerate(lengths):
        breadth = length * devices
        picked = all_ref[pl.ds(row, devices, stride=PIECE), :].astype(LOW)
        spread = jnp.where(owned(devices, length, breadth), mm(picked, one_hot(length, breadth)), 0.0)
        vec_ref[row : row + 1, 0:breadth] = column_sum(spread)
    for part in range(table_rows):
        rpe_ref[pl.ds(part, devices, stride=table_rows), :] = all_ref[
            pl.ds(len(lengths) + part, devices, stride=PIECE), :
        ]


def gather_kernel(depth, count, pieces, *refs):
    matrices, refs = refs[:count], refs[count:]
    piece_refs, refs = refs[:pieces], refs[pieces:]
    full, refs = refs[:count], refs[count:]
    vec_ref, rpe_ref = refs[:2]
    own, refs = refs[2 : 2 + count], refs[2 + count :]
    small_ref, all_ref, send, recv, local = refs
    plane = Plane(depth)
    pack_small(piece_refs, small_ref)
    for matrix, mine in zip(matrices, own):
        mine[...] = matrix[...].astype(LOW)
    plane.greet()
    gather = Gather(plane, [small_ref] + list(own), [all_ref] + list(full), (send, recv), local)
    items = count + 1
    for item in range(items):
        gather.begin(item)
    stages = (gather.over_depth, gather.over_first, gather.over_second, gather.over_core)
    for tick in range(items + len(stages) - 1):
        for late, stage in enumerate(stages):
            if 0 <= tick - late < items:
                stage(tick - late)
    for item in range(items):
        gather.sent(item)
    lengths = [piece.shape[1] for piece in piece_refs[:-1]]
    table_rows = piece_refs[-1].shape[1] // 128
    flat_ref = refs_flat(all_ref)
    unpack_small(flat_ref, lengths, table_rows, vec_ref, rpe_ref)


def refs_flat(ref):
    return ref.reshape(ref.shape[0] * ref.shape[1] * ref.shape[2], ref.shape[3])


ANYWHERE = pl.BlockSpec(memory_space=pl.ANY)


def gather_call(depth, matrices, pieces):
    chips = 4 * depth
    devices = 2 * chips
    items = len(matrices) + 1
    slots = depth - 1 + depth + 2 * depth + 4 * depth
    longest = max(piece.shape[1] for piece in pieces[:-1]) * devices
    table = pieces[-1].shape[1] * devices // 128
    result = pl.pallas_call(
        functools.partial(gather_kernel, depth, len(matrices), len(pieces)),
        out_shape=tuple(shape((chips, 2) + matrix.shape, LOW) for matrix in matrices)
        + (shape((len(pieces) - 1, longest), F32), shape((table, 128), F32)),
        in_specs=vmem(len(matrices) + len(pieces)),
        out_specs=(ANYWHERE,) * len(matrices) + tuple(vmem(2)),
        scratch_shapes=[pltpu.VMEM(matrix.shape, LOW) for matrix in matrices]
        + [
            pltpu.VMEM((PIECE, 128), F32), pltpu.VMEM((chips, 2, PIECE, 128), F32),
            pltpu.SemaphoreType.DMA((items, slots)), pltpu.SemaphoreType.DMA((items, slots)),
            pltpu.SemaphoreType.DMA((items,)),
        ],
        compiler_params=pltpu.CompilerParams(
            collective_id=0, has_side_effects=True, vmem_limit_bytes=16 * MIB
        ),
        name="gather",
    )(*matrices, *pieces)
    full = [
        piece.reshape(devices * matrix.shape[0], matrix.shape[1]) for piece, matrix in zip(result, matrices)
    ]
    return full, result[-2], result[-1]


class Scatter:
    def __init__(self, plane, given, total, from_core, from_second, from_first, from_depth, sems, local):
        self.plane, self.given, self.total = plane, given, total
        self.from_core, self.from_second = from_core, from_second
        self.from_first, self.from_depth = from_first, from_depth
        self.sems, self.local = sems, local
        depth = plane.depth
        self.first_slot = depth - 1
        self.second_slot = self.first_slot + depth
        self.core_slot = self.second_slot + 2 * depth
        self.slots = self.core_slot + 1

    def with_core(self, item):
        plane = self.plane
        return remote(
            self.given[item].at[:, 1 - plane.core], self.from_core[item], self.sems, item, self.core_slot,
            plane.sibling,
        )

    def keep_own(self, item):
        return pltpu.make_async_copy(
            self.given[item].at[:, self.plane.core], self.total[item], self.local.at[item]
        )

    def begin(self, item):
        self.with_core(item).start()
        self.keep_own(item).start()

    def to_second(self, item, index):
        plane = self.plane
        chip = plane.at(index // 2, lax.rem(index, 2), 1 - plane.second)
        return remote(
            self.total[item].at[chip], self.from_second[item].at[index], self.sems, item,
            self.second_slot + index, plane.over_second,
        )

    def to_first(self, item, z):
        plane = self.plane
        chip = plane.at(z, 1 - plane.first, plane.second)
        return remote(
            self.total[item].at[chip], self.from_first[item].at[z], self.sems, item, self.first_slot + z,
            plane.over_first,
        )

    def to_depth(self, item, index):
        plane = self.plane
        z = plane.ahead(index + 1)
        chip = plane.at(z, plane.first, plane.second)
        return remote(
            self.total[item].at[chip], self.from_depth[item].at[index], self.sems, item, index,
            plane.device(z, plane.first, plane.second),
        )

    def join(self, item, chip, piece):
        total = self.total[item]
        total[chip] = total[chip] + piece

    def over_core(self, item):
        plane = self.plane
        self.keep_own(item).wait()
        self.with_core(item).wait_recv()

        def away(index):
            chip = plane.at(index // 2, lax.rem(index, 2), 1 - plane.second)
            self.join(item, chip, self.from_core[item][chip])
            self.to_second(item, index).start()

        def stay(index):
            chip = plane.at(index // 2, lax.rem(index, 2), plane.second)
            self.join(item, chip, self.from_core[item][chip])

        each(2 * plane.depth, away)
        each(2 * plane.depth, stay)

    def over_second(self, item):
        plane = self.plane

        def away(z):
            index = 2 * z + 1 - plane.first
            self.to_second(item, index).wait_recv()
            self.join(item, plane.at(z, 1 - plane.first, plane.second), self.from_second[item][index])
            self.to_first(item, z).start()

        def stay(z):
            index = 2 * z + plane.first
            self.to_second(item, index).wait_recv()
            self.join(item, plane.at(z, plane.first, plane.second), self.from_second[item][index])

        each(plane.depth, away)
        each(plane.depth, stay)

    def over_first(self, item):
        plane = self.plane

        def away(index):
            z = plane.ahead(index + 1)
            self.to_first(item, z).wait_recv()
            self.join(item, plane.at(z, plane.first, plane.second), self.from_first[item][z])
            self.to_depth(item, index).start()

        each(plane.depth - 1, away)
        self.to_first(item, plane.z).wait_recv()
        self.join(item, plane.chip, self.from_first[item][plane.z])

    def over_depth(self, item, out_ref):
        plane = self.plane
        for index in range(plane.depth - 1):
            self.to_depth(item, index).wait_recv()
        value = self.total[item][plane.chip].astype(F32)
        for index in range(plane.depth - 1):
            value = value + self.from_depth[item][index].astype(F32)
        out_ref[...] = value

    def sent(self, item):
        def second(index):
            self.to_second(item, index).wait_send()

        def first(z):
            self.to_first(item, z).wait_send()

        def along(index):
            self.to_depth(item, index).wait_send()

        each(2 * self.plane.depth, second)
        each(self.plane.depth, first)
        each(self.plane.depth - 1, along)
        self.with_core(item).wait_send()


def pack_grads(vec_refs, rows_of, lengths, grpe_ref, flat_ref):
    devices = flat_ref.shape[0] // PIECE
    table_rows = grpe_ref.shape[0] // devices
    flat_ref[...] = jnp.zeros_like(flat_ref)
    for row, length in enumerate(lengths):
        breadth = length * devices
        value = vec_refs[rows_of[row]][row : row + 1, 0:breadth]
        spread = jnp.where(owned(devices, length, breadth), jnp.broadcast_to(value, (devices, breadth)), 0.0)
        flat_ref[pl.ds(row, devices, stride=PIECE), :] = mm2(spread, one_hot(length, breadth), 1)
    for part in range(table_rows):
        flat_ref[pl.ds(len(lengths) + part, devices, stride=PIECE), :] = grpe_ref[
            pl.ds(part, devices, stride=table_rows), :
        ]


def scatter_kernel(depth, count, lengths, *refs):
    given, refs = refs[:count], refs[count:]
    one_ref, two_ref, grpe_ref, refs = refs[0], refs[1], refs[2], refs[3:]
    outs, refs = refs[:count], refs[count:]
    pieces, refs = refs[: len(lengths) + 1], refs[len(lengths) + 1 :]
    items = count + 1
    total, refs = refs[:items], refs[items:]
    from_core, refs = refs[:items], refs[items:]
    from_second, refs = refs[:items], refs[items:]
    from_first, refs = refs[:items], refs[items:]
    from_depth, refs = refs[:items], refs[items:]
    flat_ref, sum_ref, send, recv, local = refs
    plane = Plane(depth)
    rows_of = [1] + [0] * (len(lengths) - 1)
    flat = flat_ref.reshape(2 * 4 * depth * PIECE, 128)
    pack_grads((one_ref, two_ref), rows_of, lengths, grpe_ref, flat)
    plane.greet()
    scatter = Scatter(
        plane, [flat_ref] + list(given), total, from_core, from_second, from_first, from_depth, (send, recv), local
    )
    for item in range(items):
        scatter.begin(item)
    targets = [sum_ref] + list(outs)
    stages = (
        scatter.over_core, scatter.over_second, scatter.over_first,
        lambda item: scatter.over_depth(item, targets[item]),
    )
    for tick in range(items + len(stages) - 1):
        for late, stage in enumerate(stages):
            if 0 <= tick - late < items:
                stage(tick - late)
    for item in range(items):
        scatter.sent(item)
    for row, length in enumerate(lengths):
        pieces[row][...] = sum_ref[row : row + 1, 0:length]
    table = pieces[-1]
    for part in range(table.shape[1] // 128):
        row = len(lengths) + part
        table[:, 128 * part : 128 * part + 128] = sum_ref[row : row + 1, :]


def scatter_call(depth, grads, gvec_one, gvec_two, grpe, lengths):
    chips = 4 * depth
    devices = 2 * chips
    items = len(grads) + 1
    slots = depth - 1 + depth + 2 * depth + 1
    blocks = [(grad.shape[0] // devices, grad.shape[1]) for grad in grads]
    kinds = [((PIECE, 128), F32)] + [(block, LOW) for block in blocks]
    table = grpe.shape[0] // devices * 128

    def buffers(number):
        return [pltpu.VMEM((number,) + block, kind) for block, kind in kinds]

    result = pl.pallas_call(
        functools.partial(scatter_kernel, depth, len(grads), lengths),
        out_shape=tuple(shape(block, F32) for block in blocks)
        + tuple(shape((1, length), F32) for length in lengths + (table,)),
        in_specs=[ANYWHERE] * len(grads) + vmem(3),
        out_specs=tuple(vmem(len(grads) + len(lengths) + 1)),
        scratch_shapes=buffers(chips) + buffers(chips) + buffers(2 * depth) + buffers(depth) + buffers(depth - 1)
        + [
            pltpu.VMEM((chips, 2, PIECE, 128), F32), pltpu.VMEM((PIECE, 128), F32),
            pltpu.SemaphoreType.DMA((items, slots)), pltpu.SemaphoreType.DMA((items, slots)),
            pltpu.SemaphoreType.DMA((items,)),
        ],
        compiler_params=pltpu.CompilerParams(
            collective_id=1, has_side_effects=True, vmem_limit_bytes=60 * MIB
        ),
        name="scatter",
    )(*[grad.reshape((chips, 2) + block) for grad, block in zip(grads, blocks)], gvec_one, gvec_two, grpe)
    matrices, pieces = result[: len(grads)], result[len(grads) :]
    return matrices, [piece.reshape(-1) for piece in pieces]


def plain_gather(value):
    return lax.all_gather(value.astype(LOW), "dp", axis=0, tiled=True)


def plain_scatter(value):
    return lax.psum_scatter(value.astype(F32), "dp", scatter_dimension=0, tiled=True)


def body(
    depth, tokens, cotangent, seq_lengths, random_feat, w_qkv, b_qkv, w_out, b_out, ln1_gain, ln1_bias,
    w_up, b_up, w_down, b_down, ln2_gain, ln2_bias, rpe_table,
):
    vectors = (b_qkv, b_up, b_out, ln1_gain, ln1_bias, b_down, ln2_gain, ln2_bias)
    matrices = (w_qkv, w_out, w_up, w_down)
    if depth:
        pieces = [piece.reshape(1, -1) for piece in vectors + (rpe_table,)]
        (full_qkv, full_out, full_up, full_down), vec, rpe = gather_call(depth, matrices, pieces)
    else:
        full_vectors = [plain_gather(piece).astype(F32) for piece in vectors]
        longest = max(piece.shape[0] for piece in full_vectors)
        vec = jnp.stack([jnp.pad(piece, (0, longest - piece.shape[0])) for piece in full_vectors])
        rpe = plain_gather(rpe_table).astype(F32).reshape(-1, 128)
        full_qkv, full_out, full_up, full_down = [plain_gather(piece) for piece in matrices]
    scaled, phi, low, den, ctx, ctx_low = forward_call(seq_lengths, tokens, random_feat, full_qkv, vec, rpe)
    out, g_hidden, g_ctx, d_out, d_up, d_down, gvec_one = middle_call(
        seq_lengths, tokens, cotangent, ctx_low, vec, full_out, full_up, full_down
    )
    g_tokens, d_qkv, gvec_two, grpe = backward_call(
        seq_lengths, tokens, random_feat, full_qkv, rpe, scaled, phi, low, den, ctx, g_ctx, g_hidden, vec
    )
    grads = (d_qkv, d_out, d_up, d_down)
    lengths = tuple(piece.shape[0] for piece in vectors)
    if depth:
        sums, pieces = scatter_call(depth, grads, gvec_one, gvec_two, grpe, lengths)
    else:
        gvec = gvec_one + gvec_two
        sums = [plain_scatter(grad) for grad in grads]
        devices = lax.axis_size("dp")
        pieces = [plain_scatter(gvec[row, : length * devices]) for row, length in enumerate(lengths)]
        pieces.append(plain_scatter(grpe.reshape(-1)))
    s_qkv, s_out, s_up, s_down = sums
    p_qkv, p_up, p_out, p_gain_one, p_bias_one, p_down, p_gain_two, p_bias_two, p_rpe = pieces
    return (
        out, g_tokens, s_qkv, p_qkv, s_out, p_out, p_gain_one, p_bias_one, s_up, p_up, s_down, p_down,
        p_gain_two, p_bias_two, p_rpe,
    )


def solution(mesh):
    wide, flat = P("dp", None), P("dp")
    devices = mesh.shape["dp"]
    depth = devices // 8 if devices in (16, 32) else 0
    in_specs = (
        wide, wide, wide, P(), wide, flat, wide, flat, flat, flat, wide, flat, wide, flat, flat, flat, flat,
    )
    out_specs = (
        wide, wide, wide, flat, wide, flat, flat, flat, wide, flat, wide, flat, flat, flat, flat,
    )
    return jax.shard_map(
        functools.partial(body, depth), mesh=mesh, in_specs=in_specs, out_specs=out_specs, check_vma=False
    )
```

time: 1420 us -> 311 us (0.22); the launches traced: 1400 us -> 311 us
  waiting for transfers between devices: 579 us -> 0 us
  local copies, waits for them, and re-layouts: 447 us -> 33.9 us
  Pallas kernels: 0 us -> 275 us
  matrix products: 228 us -> 0 us
  blocking collectives: 82.9 us -> 0 us
  other arithmetic: 44.8 us -> 1.26 us
  between operations: 16.3 us -> 0.7 us
    reduce_scatter x3 -> x0, waiting for transfers between devices: 378 us -> none  [the longest x1 142 us: body(): lax.psum_scatter(grad_up, 'dp', scatter_dimension=0, tiled=True)]
    pallas_call x0 -> x5, Pallas kernels: none -> 275 us  [the longest x1 97.5 us: scatter_call(): pl.pallas_call(functools.partial(scatter_kernel, depth, len(grads), lengt...]
    dot_general x100 -> x0, matrix products: 228 us -> none  [the longest x68 143 us: contract(): lax.dot_general(first_op, second_op, (((first_dim,), (second_dim,)), ((),...]
    unnamed x11 -> x0, waiting for transfers between devices: 201 us -> none
    reshape x61 -> x1, local copies, waits for them, and re-layouts: 142 us -> 0.68 us  [body(): pieces = [piece.reshape(1, -1) for piece in vectors + (rpe_table,)]]
    rev x36 -> x0, local copies, waits for them, and re-layouts: 106 us -> none  [the longest x12 82.2 us: diagonal_sums(): matrix[::-1]]
    unnamed x1 -> x0, blocking collectives: 42.5 us -> none
    all_gather x1 -> x0, blocking collectives: 40.4 us -> none  [body(): lax.all_gather(to_low(rpe_table), 'dp', axis=0, tiled=True)]
  transfers between devices with their start and end apart: 9 -> 0, of which waited for: 5 -> 0; matrix products, arithmetic and copies ran while one was open for 21% -> 0% of each run, Pallas kernels for 0% -> 0%
where the time goes in v1:
time: 311 us
  Pallas kernels  275 us (88%)
  local copies, waits for them, and re-layouts  33.9 us (11%)
    pallas_call x1, Pallas kernels, scatter_call(): pl.pallas_call(functools.partial(scatter_kernel, depth, len(grads), lengt...  97.5 us
    pallas_call x1, Pallas kernels, gather_call(): pl.pallas_call(functools.partial(gather_kernel, depth, len(matrices), len...  72.2 us
    pallas_call x1, Pallas kernels, backward_call(): pl.pallas_call(backward_kernel, out_shape=(shape((rows, breadth), F32), s...  40.9 us
    pallas_call x1, Pallas kernels, middle_call(): pl.pallas_call(middle_kernel, out_shape=(shape((rows, breadth), LOW), sha...  39.5 us
    unnamed x48, local copies, waits for them, and re-layouts  33.2 us
    pallas_call x1, Pallas kernels, forward_call(): pl.pallas_call(forward_kernel, out_shape=(shape((rows, 2 * breadth), F32)...  24.9 us

profile of v1, /device:TPU:0, one launch (start us, length us, event | category | flops | bytes accessed | tf_op | source)
XLA Modules:
  0.0 310.9 jit_solution(14639830738562727210)
XLA Ops:
  0.6 0.7 reshape.116.refs_12_
  1.3 1.0 copy-done.5
  2.3 1.0 copy-done.6
  3.3 0.9 copy-done.7
  4.2 0.9 copy-done.9
  5.1 0.7 copy-done.10
  5.7 0.7 copy-done.11
  6.4 0.7 copy-done.12
  7.0 0.7 copy-done.13
  7.7 0.7 copy-done.14
  10.3 72.2 %gather.1 = (bf16[16,2,24,2304]{3,2,1,0:T(8,128)(2,1)S(1)}, bf16[16,2,24,768]{3,2,1,0:T(8,128)(2,1)S(1)}, bf16[16,2,24,3072]{3,2,1,0:T(8,128)(2,1)S(1)}, bf16[16...) custom-call(f32[24,2304]{1,0:T(8,128)S(1)} %copy-done.7, f32[24,768]{1,0:T(8,128)S(1)} %copy-done.9, ...), custom_call_target="tpu_custom_call" | custom-call | tf_op jit(solution)/shard_map/gather/pallas_call | solution.py:741
  82.6 1.8 copy-done
  84.4 2.2 copy-done.1
  86.6 2.1 copy-done.2
  88.7 1.0 copy-done.3
  91.0 24.9 %attend.1 = (f32[512,1536]{1,0:T(8,128)}, f32[512,1536]{1,0:T(8,128)}, bf16[512,2304]{1,0:T(8,128)(2,1)}, f32[512,768]{1,0:T(8,128)}, f32[512,768]{1,0:T(8,128)}, /*index=5*/bf16[512,768]{1,0:T(8,128)(2,1)}) custom-call(s32[1,2]{1,0:T(1,128)} %seq_ref.5, bf16[512,768]{1,0:T(8,128)(2,1)} %tokens_ref.5, bf16[12,64,64]{2,1,0:T(8,128)(2,1)} %feat_ref.3, ...), custom_call_target="tpu_custom_call" | custom-call | tf_op jit(solution)/shard_map/attend/pallas_call | solution.py:436
  115.9 39.5 %feed_forward.1 = (bf16[512,768]{1,0:T(8,128)(2,1)}, f32[512,768]{1,0:T(8,128)}, f32[512,768]{1,0:T(8,128)}, bf16[768,768]{1,0:T(8,128)(2,1)}, bf16[768,3072]{1,...) custom-call(s32[1,2]{1,0:T(1,128)} %seq_ref.5, bf16[512,768]{1,0:T(8,128)(2,1)} %tokens_ref.5, ...), custom_call_target="tpu_custom_call" | custom-call | tf_op jit(solution)/shard_map/feed_forward/pallas_call | solution.py:456
  155.4 40.9 %attend_back.1 = (f32[512,768]{1,0:T(8,128)}, bf16[768,2304]{1,0:T(8,128)(2,1)}, f32[8,3072]{1,0:T(8,128)}, f32[96,128]{1,0:T(8,128)}) custom-call(s32[1,2]{1,0:T(1,128)} %seq_ref.5, bf16[512,768]{1,0:T(8,128)(2,1)} %tokens_ref.5, bf16[12,64,64]{2,1,0:T(8,128)(2,1)} %feat_ref.3, bf16[768,2304]{1,0:T(8,128)(2,1)} %bitcast.25, f32[96,128]{1,0:T(8,128)} %copy-done.8, ...), custom_call_target="tpu_custom_call" | custom-call | tf_op jit(solution)/shard_map/attend_back/pallas_call | solution.py:478
  196.3 97.5 %scatter.1 = (f32[24,2304]{1,0:T(8,128)}, f32[24,768]{1,0:T(8,128)}, f32[24,3072]{1,0:T(8,128)}, f32[96,768]{1,0:T(8,128)}, f32[1,72]{1,0:T(1,128)}, /*index=5*/...) custom-call(bf16[16,2,24,2304]{3,2,1,0:T(8,128)(2,1)} %bitcast.39, ...), custom_call_target="tpu_custom_call" | custom-call | tf_op jit(solution)/shard_map/scatter/pallas_call | solution.py:961
  293.8 1.3 reduce
  295.1 1.6 copy.44
  296.7 1.1 copy.45
  297.8 1.5 copy.46
  299.3 1.2 copy.47
  300.5 1.1 copy.48
  301.6 1.2 copy.49
  302.8 1.7 copy.50
  304.5 1.2 copy.51
  305.7 1.7 copy.52
  307.4 1.2 copy.53
  308.6 1.2 copy.54
  309.7 1.1 copy.55
  (23 shorter events, 3.2 us)
Async XLA Ops:
  1.3 1.0 copy-start.5
  2.3 1.0 copy-start.6
  3.3 0.9 copy-start.7
  4.2 0.9 copy-start.9
  5.1 0.7 copy-start.10
  5.7 0.7 copy-start.11
  6.4 0.7 copy-start.12
  7.0 0.7 copy-start.13
  7.7 0.7 copy-start.14
  8.4 0.7 copy-start.15
  9.0 0.7 copy-start.16
  9.7 0.7 copy-start.17
  82.6 1.8 copy-start
  84.4 2.2 copy-start.1
  86.6 2.1 copy-start.2
  88.7 1.0 copy-start.3
  89.8 0.6 copy-start.4
  90.4 0.6 copy-start.8
